TPU v7x, 256 devices: a whole 4x4x8 slice. The times are simulated.
256 devices in a mesh: grp: 8 (over x, core), dev: 32 (over y, z).
Axes of the slice: x: 4, y: 4, z: 8, core: 2. Of those that a mesh axis runs over, the one named last changes fastest.
Arguments:
- queries: bfloat16 [65536, 768], P(('grp', 'dev')), may hold values from -1.796875 to 1.796875
- query_slots: int32 [65536], P('grp'), may hold values from 0 to 8191, as said below
- w_res: bfloat16 [768, 768], replicated, may hold values from -0.21875 to 0.21875
- labels: bfloat16 [5120, 128, 768], P(('grp', 'dev')), may hold values from -0.71875 to 0.71875
- blocks: int32 [512, 12], P('grp'), may hold values from 0 to 5119, as said below
- positives: int32 [65536, 4], P(('grp', 'dev')), may hold values from 0 to 655359, as said below
Outputs:
- query_loss: float32 [65536], P(('grp', 'dev'))
- query_grad: bfloat16 [65536, 768], P(('grp', 'dev'))
- label_grad: bfloat16 [5120, 128, 768], P(('grp', 'dev'))
- residual_grad: bfloat16 [768, 768], replicated
Inputs may be any that keep to these rules, and one draw needn't show every extreme that they name: `query_slots`: the rows of one grp index (rows g * 256 * 32 onward) hold a permutation of 0 to 8191; a place // 256 is the dev index that owns the query's cluster, and the 256 rows of every device send exactly 8 queries to each owner. Row c lists 12 different blocks, all held by devices of the same grp index as the cluster's owner (device c // 2). The 2 clusters of one device list at most 16 distinct blocks, of which at most 1 are held by any one device; for every device's clusters some holder reaches 1. `positives`: the 4 labels of row r are different and lie in 4 different blocks listed for cluster r // 128.
All inputs are finite; a program needn't handle non-finite values.
Results may differ from a plain program's by a relative error of at most 0.0047.
The roundings to bfloat16 on the way count: a program that leaves them out, or rounds other values in their place, can miss the bound.
Values may be sent and summed in bfloat16 or wider, within the bound.
No kernel may reach another device: no remote copies, remote signals or barrier semaphores. Data moves between devices by JAX's collectives and lax.ppermute only.
A program may use at most 128 MiB of HBM per device.

v0:
```python
from functools import partial
import jax
import jax.numpy as jnp
from jax import lax
from jax.sharding import PartitionSpec as P

BLK = 128
CSIZE = 128
SHORT = 12
NPOS = 4
POOL = 16
BLK_DEV = 20


def activate(values):
    return jax.nn.gelu(values, approximate=True)


def activate_slope(values):
    return jax.vjp(activate, values)[1](jnp.ones_like(values))[0]


def request_plan(listed, owner_base, peer_count, per_owner):
    owners = listed // BLK_DEV - owner_base
    within = listed % BLK_DEV
    positions = jnp.arange(listed.shape[0], dtype=jnp.int32)
    earlier = positions[None, :] < positions[:, None]
    same_block = listed[:, None] == listed[None, :]
    leading = jnp.logical_not(jnp.any(same_block & earlier, axis=1))
    first_seen = jnp.argmax(same_block, axis=1)
    same_owner = owners[:, None] == owners[None, :]
    ranking = jnp.sum(same_owner & earlier & leading[None, :], axis=1)
    own_place = owners * per_owner + ranking
    placed = own_place[first_seen]
    target = jnp.where(leading, own_place, peer_count * per_owner)
    request_table = (
        jnp.full((peer_count * per_owner,), -1, jnp.int32).at[target].set(within, mode="drop")
    )
    return (placed, request_table.reshape(peer_count, per_owner))


def local(queries, query_slots, w_res, labels, blocks, positives):
    peer_count = lax.axis_size("dev")
    groups = lax.axis_size("grp")
    own_index = lax.axis_index("dev")
    group_index = lax.axis_index("grp")
    rows_dev = queries.shape[0]
    feature_width = queries.shape[1]
    per_peer = rows_dev // peer_count
    clusters_dev = rows_dev // CSIZE
    per_owner = (POOL + peer_count - 1) // peer_count
    slots_total = peer_count * per_owner
    own_slots = lax.dynamic_slice_in_dim(query_slots, own_index * rows_dev, rows_dev)
    outbound = jnp.argsort(own_slots // rows_dev, stable=True)
    slot_grid = query_slots.reshape(peer_count, rows_dev)
    grid_order = jnp.argsort(slot_grid // rows_dev, axis=1, stable=True)
    grid_sorted = jnp.take_along_axis(slot_grid, grid_order, axis=1)
    incoming = (
        lax.dynamic_slice_in_dim(grid_sorted, own_index * per_peer, per_peer, 1).reshape(rows_dev)
        - own_index * rows_dev
    )
    arrange = jnp.argsort(incoming)
    pre_act = jnp.dot(queries, w_res, preferred_element_type=jnp.float32)
    payload = (queries.astype(jnp.float32) + activate(pre_act)).astype(jnp.bfloat16)
    arrived = lax.all_to_all(
        payload[outbound].reshape(peer_count, per_peer, feature_width),
        "dev",
        split_axis=0,
        concat_axis=0,
        tiled=True,
    )
    arrived = arrived.reshape(rows_dev, feature_width)[arrange]
    listed_all = blocks.reshape(peer_count, clusters_dev * SHORT)
    owner_base = group_index * peer_count
    planner = partial(
        request_plan, owner_base=owner_base, peer_count=peer_count, per_owner=per_owner
    )
    places_all, tables_all = jax.vmap(planner)(listed_all)
    own_places = places_all[own_index].reshape(clusters_dev, SHORT)
    wanted_flat = tables_all[:, own_index, :].reshape(-1)
    block_range = jnp.arange(labels.shape[0], dtype=jnp.int32)
    reply_pick = (wanted_flat[:, None] == block_range[None, :]).astype(jnp.bfloat16)
    reply_blocks = jnp.einsum(
        "sb,bjd->sjd", reply_pick, labels, preferred_element_type=jnp.float32
    ).astype(jnp.bfloat16)
    fetched = lax.all_to_all(
        reply_blocks.reshape(peer_count, per_owner, BLK, feature_width),
        "dev",
        split_axis=0,
        concat_axis=0,
        tiled=True,
    )
    fetched = fetched.reshape(slots_total, BLK, feature_width)
    listed_ids = listed_all[own_index].reshape(clusters_dev, SHORT)
    cluster_rows = arrived.reshape(clusters_dev, CSIZE, feature_width)
    wanted_pos = positives.reshape(clusters_dev, CSIZE, NPOS)
    offsets = jnp.arange(BLK, dtype=jnp.int32)
    slot_range = jnp.arange(slots_total, dtype=jnp.int32)
    place_pick = (own_places[:, :, None] == slot_range[None, None, :]).astype(jnp.bfloat16)

    def per_cluster(running, pieces):
        rows_here, pick_here, ids_here, pos_here = pieces
        chosen = jnp.einsum(
            "ks,sjd->kjd", pick_here, fetched, preferred_element_type=jnp.float32
        ).astype(jnp.bfloat16)
        logits = jnp.einsum("qd,kjd->qkj", rows_here, chosen, preferred_element_type=jnp.float32)
        label_ids = ids_here[:, None] * BLK + offsets[None, :]
        targets = jnp.any(
            label_ids[None, :, :, None] == pos_here[:, None, None, :], axis=-1
        ).astype(jnp.float32)
        loss_rows = jnp.mean(jax.nn.softplus(logits) - targets * logits, axis=(1, 2))
        errors = (jax.nn.sigmoid(logits) - targets).astype(jnp.bfloat16)
        grad_rows = jnp.einsum(
            "qkj,kjd->qd", errors, chosen, preferred_element_type=jnp.float32
        ).astype(jnp.bfloat16)
        terms_cluster = jnp.einsum(
            "qkj,qd->kjd", errors, rows_here, preferred_element_type=jnp.float32
        )
        return (running, (loss_rows, grad_rows, terms_cluster))

    pieces = (cluster_rows, place_pick, listed_ids, wanted_pos)
    running, (losses, grads, terms) = lax.scan(per_cluster, jnp.zeros((), jnp.float32), pieces)
    selector = (own_places.reshape(-1)[:, None] == slot_range[None, :]).astype(jnp.float32)
    summed = jnp.einsum(
        "rs,rjd->sjd",
        selector,
        terms.reshape(-1, BLK, feature_width),
        precision=lax.Precision.HIGHEST,
        preferred_element_type=jnp.float32,
    )
    returned_grads = lax.all_to_all(
        summed.astype(jnp.bfloat16).reshape(peer_count, per_owner, BLK, feature_width),
        "dev",
        split_axis=0,
        concat_axis=0,
        tiled=True,
    )
    returned_grads = returned_grads.reshape(slots_total, BLK, feature_width)
    label_grad = jnp.einsum(
        "sb,sjd->bjd", reply_pick, returned_grads, preferred_element_type=jnp.float32
    ).astype(jnp.bfloat16)
    cluster_grad = grads.reshape(rows_dev, feature_width)
    returned = lax.all_to_all(
        cluster_grad[incoming].reshape(peer_count, per_peer, feature_width),
        "dev",
        split_axis=0,
        concat_axis=0,
        tiled=True,
    )
    restored = returned.reshape(rows_dev, feature_width)[jnp.argsort(outbound)]
    grad_pre = (restored.astype(jnp.float32) * activate_slope(pre_act)).astype(jnp.bfloat16)
    back_term = jnp.einsum("qe,de->qd", grad_pre, w_res, preferred_element_type=jnp.float32)
    query_grad = (restored.astype(jnp.float32) + back_term).astype(jnp.bfloat16)
    weight_term = jnp.einsum("qd,qe->de", queries, grad_pre, preferred_element_type=jnp.float32)
    weight_sum = lax.psum(weight_term, ("grp", "dev"))
    scale_factor = float(rows_dev * peer_count * groups) ** (-0.5)
    return (
        losses.reshape(rows_dev),
        query_grad,
        label_grad,
        (weight_sum * scale_factor).astype(jnp.bfloat16),
    )


def solution(mesh):
    in_specs = (
        P(("grp", "dev"), None),
        P("grp"),
        P(),
        P(("grp", "dev"), None, None),
        P("grp", None),
        P(("grp", "dev"), None),
    )
    out_specs = (P(("grp", "dev")), P(("grp", "dev"), None), P(("grp", "dev"), None, None), P())
    return jax.shard_map(local, mesh=mesh, in_specs=in_specs, out_specs=out_specs, check_vma=False)
```

profile of v0, /device:TPU:2, one launch (start us, length us, event | category | flops | bytes accessed | tf_op | source)
XLA Modules:
  0.0 643.6 jit_solution(3490546229624405968)
XLA Ops:
  7.2 0.9 and_select_fusion
  8.1 3.2 sort.65
  11.2 2.6 add_convert_fusion
  13.8 1.9 gather_fusion
  15.8 11.5 %all-to-all-start = ((bf16[32,8,768]{2,1,0:T(8,128)(2,1)}), bf16[32,8,768]{2,1,0:T(8,128)(2,1)S(1)}, u32[]{:S(2)}, u32[]{:S(2)}) async-start(bf16[32,8,768]{2,1,0:T(8,128)(2,1)} %bitcast), calls=%async_computation | async-start | bytes 786432 | tf_op jit(solution)/shard_map/all_to_all | solution.py:65
  27.3 0.1 copy.100
  27.4 0.1 copy.107
  27.5 0.1 and.80
  27.6 0.1 copy.110
  27.7 0.1 copy.108
  28.1 0.2 fusion.41
  28.4 0.1 reshape.326
  28.5 0.2 convert_reduce_fusion
  28.7 0.1 reshape.324
  28.9 37.8 %scatter_fusion = s32[32,32]{1,0:T(8,128)S(1)} fusion(s32[32,32]{1,0:T(8,128)S(1)} %broadcast_in_dim.65, s32[768]{0:T(1024)S(1)} %reshape.324, s32[768]{0:T(1024)S(1)} %reshape.326), kind=kCustom, calls=%fused_computation.6 | custom fusion | bytes 15360 | tf_op jit(solution)/shard_map/vmap()/scatter | solution.py:37
  66.7 0.2 dynamic-slice_reduce_fusion
  66.9 5.4 convert_bitcast_fusion.1
  72.3 6.3 copy.115
  78.5 10.0 %all-to-all-start.1 = ((bf16[32,1,128,768]{3,2,1,0:T(8,128)(2,1)}), bf16[32,1,128,768]{3,2,1,0:T(8,128)(2,1)}, u32[]{:S(2)}, u32[]{:S(2)}) async-start(bf16[32,1,128,768]{3,2,1,0:T(8,128)(2,1)} %copy.115), calls=%async_computation.1 | async-start | bytes 12582912 | tf_op jit(solution)/shard_map/all_to_all | solution.py:86
  88.7 0.6 add_select_fusion
  89.3 0.6 iota.54
  90.0 1.3 compare_reduce_fusion.1
  91.3 0.1 reshape.318
  91.4 5.3 gather_fusion.5
  96.8 0.1 eq.96
  97.1 0.8 fusion.43
  97.9 65.0 %gather_fusion.4 = s32[8192]{0:T(1024)S(1)} fusion(s32[32,256]{1,0:T(8,128)S(1)} %reshape.266, s32[8192]{0:T(1024)S(1)} %bitcast.111), kind=kCustom, calls=%fused_computation.4 | custom fusion | bytes 131072 | tf_op jit(solution)/shard_map/jit(take_along_axis)/gather | solution.py:57
  163.0 0.1 fusion.45
  163.1 0.1 sub.83
  163.2 0.1 sub.76
  163.3 3.2 sort.67
  166.5 1.2 gather_fusion.1
  167.7 60.9 %all-to-all-done.1 = bf16[32,1,128,768]{3,2,1,0:T(8,128)(2,1)} async-done(((bf16[32,1,128,768]{3,2,1,0:T(8,128)(2,1)}), bf16[32,1,128,768]{3,2,1,0:T(8,128)(2,1)}, u32[]{:S(2)}, u32[]{:S(2)}) %all-to-all-start.1) | async-done | bytes 6291488 | tf_op jit(solution)/shard_map/all_to_all | solution.py:86
  228.5 9.0 %copy.116 = bf16[32,128,768]{2,0,1:T(8,128)(2,1)} copy(bf16[32,128,768]{2,1,0:T(8,128)(2,1)} %bitcast.9) | data formatting | bytes 12582912
  237.5 22.7 %while.15 = (s32[]{:T(128)}, f32[2,128]{1,0:T(2,128)S(1)}, bf16[2,128,768]{2,1,0:T(8,128)(2,1)S(1)}, f32[2,12,128,768]{3,2,1,0:T(8,128)}, bf16[2,128,768]{2,1,0:...) while((s32[]{:T(128)}, f32[2,128]{1,0:T(2,128)S(1)}, ...), condition=%wide.region_10.11_spmd.clone, body=%wide.region_7.10_spmd.clone.sunk | while | flops 988628480 | bytes 24667932 | solution.py:122
  237.6 0.5 compare_reduce_fusion.3
  238.1 0.3 copy.148
  238.4 3.8 fusion.90
  242.2 1.5 fusion.91
  243.7 1.6 fusion.92
  245.3 0.6 subtract_reduce_fusion.2
  245.9 2.9 bitcast_dynamic-update-slice_fusion.2
  248.9 0.5 compare_reduce_fusion.3
  249.4 0.3 copy.148
  249.7 3.8 fusion.90
  253.5 1.5 fusion.91
  255.0 1.6 fusion.92
  256.6 0.6 subtract_reduce_fusion.2
  257.2 2.9 bitcast_dynamic-update-slice_fusion.2
  260.2 1.9 gather_fusion.2
  262.1 8.2 %all-to-all-start.2 = ((bf16[32,8,768]{2,1,0:T(8,128)(2,1)}), bf16[32,8,768]{2,1,0:T(8,128)(2,1)S(1)}, u32[]{:S(2)}, u32[]{:S(2)}) async-start(bf16[32,8,768]{2,1,0:T(8,128)(2,1)} %bitcast.14), calls=%async_computation.2 | async-start | bytes 786432 | tf_op jit(solution)/shard_map/all_to_all | solution.py:143
  270.3 14.7 %convert_bitcast_fusion = bf16[32,1,128,768]{3,0,2,1:T(8,128)(2,1)S(1)} fusion(f32[24,128,768]{2,1,0:T(8,128)} %bitcast.115, s32[24]{0:T(128)S(1)} %get-tuple-element.171), kind=kOutput, calls=%fused_computation.42 | convolution fusion | flops 909116160 | bytes 15728736 | tf_op jit(solution)/shard_map/rs,rjd->sjd/dot_general | solution.py:124
  285.0 6.2 copy.118
  291.3 10.2 %all-to-all-start.3 = ((bf16[32,1,128,768]{3,2,1,0:T(8,128)(2,1)}), bf16[32,1,128,768]{3,2,1,0:T(8,128)(2,1)}, u32[]{:S(2)}, u32[]{:S(2)}) async-start(bf16[32,1,128,768]{3,2,1,0:T(8,128)(2,1)} %copy.118), calls=%async_computation.3 | async-start | bytes 12582912 | tf_op jit(solution)/shard_map/all_to_all | solution.py:131
  301.4 0.3 all-reduce.2.cloned.1.call-start
  301.7 3.2 sort.68
  304.9 1.2 gather_fusion.3
  306.1 2.4 convolution_bitcast_fusion.1
  308.5 1.6 fusion.33
  310.1 312.4 %all-reduce.2.cloned.1.call-done = f32[768,768]{0,1:T(8,128)} async-done(((f32[768,768]{0,1:T(8,128)}), f32[768,768]{0,1:T(8,128)}) %all-reduce.2.cloned.1.call-update) | async-done | bytes 2359312 | tf_op jit(solution)/shard_map/psum | solution.py:155
  622.6 1.8 multiply_convert_fusion
  624.4 1.5 copy.121
  625.9 7.9 %fusion.30 = bf16[20,128,768]{2,0,1:T(8,128)(2,1)S(1)} fusion(bf16[32,1,128,768]{3,2,1,0:T(8,128)(2,1)} %all-to-all-done.3, s32[32]{0:T(128)S(1)} %dynamic-slice_reduce_fusion), kind=kOutput, calls=%fused_computation.46 | convolution fusion | flops 127795840 | bytes 10223744 | tf_op jit(solution)/shard_map/sb,sjd->bjd/dot_general | solution.py:139
  633.8 2.8 copy.120
  (72 shorter events, 1.4 us)
Async XLA Ops:
  7.2 4.1 copy-start
  7.2 20.1 %copy-start.2 = (s32[64,12]{0,1:T(8,128)S(1)}, s32[64,12]{0,1:T(8,128)}, u32[]{:S(2)}) copy-start(s32[64,12]{0,1:T(8,128)} %param.12) | copy-start | bytes 9220
  15.8 62.8 %all-to-all-start = ((bf16[32,8,768]{2,1,0:T(8,128)(2,1)}), bf16[32,8,768]{2,1,0:T(8,128)(2,1)S(1)}, u32[]{:S(2)}, u32[]{:S(2)}) async-start(bf16[32,8,768]{2,1,0:T(8,128)(2,1)} %bitcast), calls=%async_computation | async-start | bytes 786432 | tf_op jit(solution)/shard_map/all_to_all | solution.py:65
  78.5 10.1 %copy-start.3 = (s32[8192]{0:T(1024)S(1)}, s32[8192]{0:T(1024)}, u32[]{:S(2)}) copy-start(s32[8192]{0:T(1024)} %param.9) | copy-start | bytes 98308
  78.5 150.0 %all-to-all-start.1 = ((bf16[32,1,128,768]{3,2,1,0:T(8,128)(2,1)}), bf16[32,1,128,768]{3,2,1,0:T(8,128)(2,1)}, u32[]{:S(2)}, u32[]{:S(2)}) async-start(bf16[32,1,128,768]{3,2,1,0:T(8,128)(2,1)} %copy.115), calls=%async_computation.1 | async-start | bytes 12582912 | tf_op jit(solution)/shard_map/all_to_all | solution.py:86
  88.6 8.5 %sort.70.cloned.1.call-start = ((), (), s32[]{:S(2)}) async-start(), calls=%async_computation.5 | async-start | bytes 196640 | tf_op jit(solution)/shard_map/jit(argsort)/sort | solution.py:56
  97.9 65.0 %copy-start.1 = (s32[32,256]{1,0:T(8,128)S(1)}, s32[32,256]{1,0:T(8,128)}, u32[]{:S(2)}) copy-start(s32[32,256]{1,0:T(8,128)} %get-tuple-element.64) | copy-start | bytes 98308
  228.5 9.0 %copy-start.4 = (s32[256,4]{0,1:T(4,128)S(1)}, s32[256,4]{0,1:T(4,128)}, u32[]{:S(2)}) copy-start(s32[256,4]{0,1:T(4,128)} %param.13) | copy-start | bytes 12292
  260.2 24.9 %copy-start.6 = (f32[2,128]{1,0:T(2,128)}, f32[2,128]{1,0:T(2,128)S(1)}, u32[]{:S(2)}) copy-start(f32[2,128]{1,0:T(2,128)S(1)} %get-tuple-element.67) | copy-start | bytes 3076
  262.1 29.2 %all-to-all-start.2 = ((bf16[32,8,768]{2,1,0:T(8,128)(2,1)}), bf16[32,8,768]{2,1,0:T(8,128)(2,1)S(1)}, u32[]{:S(2)}, u32[]{:S(2)}) async-start(bf16[32,8,768]{2,1,0:T(8,128)(2,1)} %bitcast.14), calls=%async_computation.2 | async-start | bytes 786432 | tf_op jit(solution)/shard_map/all_to_all | solution.py:143
  291.3 14.8 %copy-start.5 = (bf16[256,768]{1,0:T(8,128)(2,1)S(1)}, bf16[256,768]{1,0:T(8,128)(2,1)}, u32[]{:S(2)}) copy-start(bf16[256,768]{1,0:T(8,128)(2,1)} %param.8) | copy-start | bytes 1179652
  291.3 14.8 %copy-start.7 = (f32[256,768]{1,0:T(8,128)S(1)}, f32[256,768]{1,0:T(8,128)}, u32[]{:S(2)}) copy-start(f32[256,768]{1,0:T(8,128)} %get-tuple-element.176) | copy-start | bytes 2359300
  291.3 334.6 %all-to-all-start.3 = ((bf16[32,1,128,768]{3,2,1,0:T(8,128)(2,1)}), bf16[32,1,128,768]{3,2,1,0:T(8,128)(2,1)}, u32[]{:S(2)}, u32[]{:S(2)}) async-start(bf16[32,1,128,768]{3,2,1,0:T(8,128)(2,1)} %copy.118), calls=%async_computation.3 | async-start | bytes 12582912 | tf_op jit(solution)/shard_map/all_to_all | solution.py:131
  301.4 321.1 %all-reduce.2.cloned.1.call-start = ((), (), s32[]{:S(2)}) async-start(), calls=%async_computation.4 | async-start | bytes 4718592 | tf_op jit(solution)/shard_map/psum | solution.py:155
Sparse Core Ops, SparseCore 0:
  92.3 2.5 sort.72.cloned.1.call-done
  308.6 313.9 all-reduce.1
  (1 shorter events, 0.0 us)
where the time goes:
time: 652 us; the launch traced here: 644 us
  waiting for transfers between devices  373 us (57%)
  local copies, waits for them, and re-layouts  143 us (22%)
  matrix products  54.2 us (8%)
  starting transfers between devices  40.1 us (6%)
  other arithmetic  17.9 us (3%)
  between operations  14.6 us (2%)
    psum x1, waiting for transfers between devices, local(): weight_sum = lax.psum(weight_term, ('grp', 'dev'))  312 us
    gather x2, local copies, waits for them, and re-layouts, local(): grid_sorted = jnp.take_along_axis(slot_grid, grid_order, axis=1)  65 us
    all_to_all x1, waiting for transfers between devices, local(): lax.all_to_all(reply_blocks.reshape(peer_count, per_owner, BLK, feature_w...  60.9 us
    scatter x3, local copies, waits for them, and re-layouts, request_plan(): jnp.full((peer_count * per_owner,), -1, jnp.int32).at[target]  38 us
    dot_general x1, matrix products, local(): jnp.einsum('rs,rjd->sjd', selector, terms.reshape(-1, BLK, feature_width)...  14.7 us
    unnamed x22, local copies, waits for them, and re-layouts  13.4 us
  transfers between devices with their start and end apart: 5, of which 2 were waited for; matrix products, arithmetic and copies ran while one was open for 25% of the time, Pallas kernels for 0%

commit v1 on v0

--- a/solution.py
+++ b/solution.py
@@ -10,6 +10,10 @@
 NPOS = 4
 POOL = 16
 BLK_DEV = 20
+
+
+def _list_digits(xs):
+    return lax.psum(lax.psum(xs, "grp"), "dev")
 
 
 def activate(values):
@@ -152,7 +156,7 @@
     back_term = jnp.einsum("qe,de->qd", grad_pre, w_res, preferred_element_type=jnp.float32)
     query_grad = (restored.astype(jnp.float32) + back_term).astype(jnp.bfloat16)
     weight_term = jnp.einsum("qd,qe->de", queries, grad_pre, preferred_element_type=jnp.float32)
-    weight_sum = lax.psum(weight_term, ("grp", "dev"))
+    weight_sum = _list_digits(weight_term)
     scale_factor = float(rows_dev * peer_count * groups) ** (-0.5)
     return (
         losses.reshape(rows_dev),

time: 652 us -> 603 us (0.925)
  waiting for transfers between devices: 373 us -> 325 us
    psum x1 -> x2, waiting for transfers between devices: 312 us -> 264 us  [_list_digits(): return lax.psum(lax.psum(xs, 'grp'), 'dev')]
  transfers between devices with their start and end apart: 5 -> 6, of which waited for: 2 -> 3; matrix products, arithmetic and copies ran while one was open for 25% -> 27% of each run, Pallas kernels for 0% -> 0%
where the time goes in v1:
time: 603 us; the launch traced here: 595 us
  waiting for transfers between devices  325 us (54%)
  local copies, waits for them, and re-layouts  143 us (24%)
  matrix products  54.2 us (9%)
  starting transfers between devices  40.2 us (7%)
  other arithmetic  17.9 us (3%)
  between operations  14.3 us (2%)
    psum x2, waiting for transfers between devices, _list_digits(): return lax.psum(lax.psum(xs, 'grp'), 'dev')  264 us
    gather x2, local copies, waits for them, and re-layouts, local(): grid_sorted = jnp.take_along_axis(slot_grid, grid_order, axis=1)  65 us
    all_to_all x1, waiting for transfers between devices, local(): lax.all_to_all(reply_blocks.reshape(peer_count, per_owner, BLK, feature_w...  60.9 us
    scatter x3, local copies, waits for them, and re-layouts, request_plan(): jnp.full((peer_count * per_owner,), -1, jnp.int32).at[target]  38 us
    dot_general x1, matrix products, local(): jnp.einsum('rs,rjd->sjd', selector, terms.reshape(-1, BLK, feature_width)...  14.7 us
    unnamed x22, local copies, waits for them, and re-layouts  13.4 us
  transfers between devices with their start and end apart: 6, of which 3 were waited for; matrix products, arithmetic and copies ran while one was open for 27% of the time, Pallas kernels for 0%

profile of v1, /device:TPU:2, one launch (start us, length us, event | category | flops | bytes accessed | tf_op | source)
XLA Modules:
  0.0 595.1 jit_solution(5964970896359810605)
XLA Ops:
  7.2 0.9 and_select_fusion
  8.1 3.2 sort.65
  11.2 2.6 add_convert_fusion
  13.8 1.9 gather_fusion
  15.8 11.5 %all-to-all-start = ((bf16[32,8,768]{2,1,0:T(8,128)(2,1)}), bf16[32,8,768]{2,1,0:T(8,128)(2,1)S(1)}, u32[]{:S(2)}, u32[]{:S(2)}) async-start(bf16[32,8,768]{2,1,0:T(8,128)(2,1)} %bitcast), calls=%async_computation | async-start | bytes 786432 | tf_op jit(solution)/shard_map/all_to_all | solution.py:69
  27.3 0.1 copy.100
  27.4 0.1 copy.107
  27.5 0.1 and.80
  27.6 0.1 copy.110
  27.7 0.1 copy.108
  28.1 0.2 fusion.41
  28.4 0.1 reshape.326
  28.5 0.2 convert_reduce_fusion
  28.7 0.1 reshape.324
  28.9 37.8 %scatter_fusion = s32[32,32]{1,0:T(8,128)S(1)} fusion(s32[32,32]{1,0:T(8,128)S(1)} %broadcast_in_dim.65, s32[768]{0:T(1024)S(1)} %reshape.324, s32[768]{0:T(1024)S(1)} %reshape.326), kind=kCustom, calls=%fused_computation.6 | custom fusion | bytes 15360 | tf_op jit(solution)/shard_map/vmap()/scatter | solution.py:41
  66.7 0.2 dynamic-slice_reduce_fusion
  66.9 5.4 convert_bitcast_fusion.1
  72.3 6.3 %copy.115 = bf16[32,1,128,768]{3,2,1,0:T(8,128)(2,1)} copy(bf16[32,1,128,768]{3,0,2,1:T(8,128)(2,1)S(1)} %convert_bitcast_fusion.1) | data formatting | bytes 12582912 | tf_op jit(solution)/shard_map/reshape | solution.py:91
  78.5 10.0 %all-to-all-start.1 = ((bf16[32,1,128,768]{3,2,1,0:T(8,128)(2,1)}), bf16[32,1,128,768]{3,2,1,0:T(8,128)(2,1)}, u32[]{:S(2)}, u32[]{:S(2)}) async-start(bf16[32,1,128,768]{3,2,1,0:T(8,128)(2,1)} %copy.115), calls=%async_computation.1 | async-start | bytes 12582912 | tf_op jit(solution)/shard_map/all_to_all | solution.py:90
  88.7 0.6 add_select_fusion
  89.3 0.6 iota.54
  90.0 1.3 compare_reduce_fusion.1
  91.3 0.1 reshape.318
  91.4 5.3 gather_fusion.5
  97.1 0.8 fusion.43
  97.9 65.0 %gather_fusion.4 = s32[8192]{0:T(1024)S(1)} fusion(s32[32,256]{1,0:T(8,128)S(1)} %reshape.266, s32[8192]{0:T(1024)S(1)} %bitcast.111), kind=kCustom, calls=%fused_computation.4 | custom fusion | bytes 131072 | tf_op jit(solution)/shard_map/jit(take_along_axis)/gather | solution.py:61
  163.0 0.1 fusion.45
  163.1 0.1 sub.83
  163.2 0.1 sub.76
  163.3 3.2 sort.67
  166.5 1.2 gather_fusion.1
  167.7 60.9 %all-to-all-done.1 = bf16[32,1,128,768]{3,2,1,0:T(8,128)(2,1)} async-done(((bf16[32,1,128,768]{3,2,1,0:T(8,128)(2,1)}), bf16[32,1,128,768]{3,2,1,0:T(8,128)(2,1)}, u32[]{:S(2)}, u32[]{:S(2)}) %all-to-all-start.1) | async-done | bytes 6291488 | tf_op jit(solution)/shard_map/all_to_all | solution.py:90
  228.5 9.0 %copy.116 = bf16[32,128,768]{2,0,1:T(8,128)(2,1)} copy(bf16[32,128,768]{2,1,0:T(8,128)(2,1)} %bitcast.9) | data formatting | bytes 12582912
  237.5 22.7 %while.15 = (s32[]{:T(128)}, f32[2,128]{1,0:T(2,128)S(1)}, bf16[2,128,768]{2,1,0:T(8,128)(2,1)S(1)}, f32[2,12,128,768]{3,2,1,0:T(8,128)}, bf16[2,128,768]{2,1,0:...) while((s32[]{:T(128)}, f32[2,128]{1,0:T(2,128)S(1)}, ...), condition=%wide.region_10.11_spmd.clone, body=%wide.region_7.10_spmd.clone.sunk | while | flops 988628480 | bytes 24667932 | solution.py:126
  237.6 0.5 compare_reduce_fusion.3
  238.1 0.3 copy.148
  238.4 3.8 fusion.90
  242.2 1.5 fusion.91
  243.7 1.6 fusion.92
  245.3 0.6 subtract_reduce_fusion.2
  245.9 2.9 bitcast_dynamic-update-slice_fusion.2
  248.9 0.5 compare_reduce_fusion.3
  249.4 0.3 copy.148
  249.7 3.8 fusion.90
  253.5 1.5 fusion.91
  255.0 1.6 fusion.92
  256.6 0.6 subtract_reduce_fusion.2
  257.2 2.9 bitcast_dynamic-update-slice_fusion.2
  260.2 1.9 gather_fusion.2
  262.1 8.2 %all-to-all-start.2 = ((bf16[32,8,768]{2,1,0:T(8,128)(2,1)}), bf16[32,8,768]{2,1,0:T(8,128)(2,1)S(1)}, u32[]{:S(2)}, u32[]{:S(2)}) async-start(bf16[32,8,768]{2,1,0:T(8,128)(2,1)} %bitcast.14), calls=%async_computation.2 | async-start | bytes 786432 | tf_op jit(solution)/shard_map/all_to_all | solution.py:147
  270.3 14.7 %convert_bitcast_fusion = bf16[32,1,128,768]{3,0,2,1:T(8,128)(2,1)S(1)} fusion(f32[24,128,768]{2,1,0:T(8,128)} %bitcast.115, s32[24]{0:T(128)S(1)} %get-tuple-element.171), kind=kOutput, calls=%fused_computation.42 | convolution fusion | flops 909116160 | bytes 15728736 | tf_op jit(solution)/shard_map/rs,rjd->sjd/dot_general | solution.py:128
  285.0 6.2 %copy.118 = bf16[32,1,128,768]{3,2,1,0:T(8,128)(2,1)} copy(bf16[32,1,128,768]{3,0,2,1:T(8,128)(2,1)S(1)} %convert_bitcast_fusion) | data formatting | bytes 12582912 | tf_op jit(solution)/shard_map/reshape | solution.py:136
  291.3 10.2 %all-to-all-start.3 = ((bf16[32,1,128,768]{3,2,1,0:T(8,128)(2,1)}), bf16[32,1,128,768]{3,2,1,0:T(8,128)(2,1)}, u32[]{:S(2)}, u32[]{:S(2)}) async-start(bf16[32,1,128,768]{3,2,1,0:T(8,128)(2,1)} %copy.118), calls=%async_computation.3 | async-start | bytes 12582912 | tf_op jit(solution)/shard_map/all_to_all | solution.py:135
  301.4 0.3 all-reduce.3.cloned.1.call-start
  301.7 3.2 sort.68
  304.9 1.2 gather_fusion.3
  306.1 2.4 convolution_bitcast_fusion.1
  308.5 72.1 %all-reduce.3.cloned.1.call-done = f32[768,768]{0,1:T(8,128)} async-done(((f32[768,768]{0,1:T(8,128)}), f32[768,768]{0,1:T(8,128)}) %all-reduce.3.cloned.1.call-update) | async-done | bytes 2359312 | tf_op jit(solution)/shard_map/psum | solution.py:16
  380.7 1.6 fusion.33
  382.3 192.0 %all-reduce.5.cloned.1.call-done = f32[768,768]{0,1:T(8,128)} async-done(((f32[768,768]{0,1:T(8,128)}), f32[768,768]{0,1:T(8,128)}) %all-reduce.5.cloned.1.call-update) | async-done | bytes 2359312 | tf_op jit(solution)/shard_map/psum | solution.py:16
  574.3 1.8 multiply_convert_fusion
  576.2 1.5 copy.121
  577.6 7.9 %fusion.30 = bf16[20,128,768]{2,0,1:T(8,128)(2,1)S(1)} fusion(bf16[32,1,128,768]{3,2,1,0:T(8,128)(2,1)} %all-to-all-done.3, s32[32]{0:T(128)S(1)} %dynamic-slice_reduce_fusion), kind=kOutput, calls=%fused_computation.46 | convolution fusion | flops 127795840 | bytes 10223744 | tf_op jit(solution)/shard_map/sb,sjd->bjd/dot_general | solution.py:143
  585.5 2.8 copy.120
  (75 shorter events, 1.5 us)
Async XLA Ops:
  7.2 4.1 copy-start
  7.2 20.1 %copy-start.2 = (s32[64,12]{0,1:T(8,128)S(1)}, s32[64,12]{0,1:T(8,128)}, u32[]{:S(2)}) copy-start(s32[64,12]{0,1:T(8,128)} %param.12) | copy-start | bytes 9220
  15.8 62.8 %all-to-all-start = ((bf16[32,8,768]{2,1,0:T(8,128)(2,1)}), bf16[32,8,768]{2,1,0:T(8,128)(2,1)S(1)}, u32[]{:S(2)}, u32[]{:S(2)}) async-start(bf16[32,8,768]{2,1,0:T(8,128)(2,1)} %bitcast), calls=%async_computation | async-start | bytes 786432 | tf_op jit(solution)/shard_map/all_to_all | solution.py:69
  78.5 10.1 %copy-start.3 = (s32[8192]{0:T(1024)S(1)}, s32[8192]{0:T(1024)}, u32[]{:S(2)}) copy-start(s32[8192]{0:T(1024)} %param.9) | copy-start | bytes 98308
  78.5 150.0 %all-to-all-start.1 = ((bf16[32,1,128,768]{3,2,1,0:T(8,128)(2,1)}), bf16[32,1,128,768]{3,2,1,0:T(8,128)(2,1)}, u32[]{:S(2)}, u32[]{:S(2)}) async-start(bf16[32,1,128,768]{3,2,1,0:T(8,128)(2,1)} %copy.115), calls=%async_computation.1 | async-start | bytes 12582912 | tf_op jit(solution)/shard_map/all_to_all | solution.py:90
  88.6 8.5 %sort.70.cloned.1.call-start = ((), (), s32[]{:S(2)}) async-start(), calls=%async_computation.6 | async-start | bytes 196640 | tf_op jit(solution)/shard_map/jit(argsort)/sort | solution.py:60
  97.9 65.0 %copy-start.1 = (s32[32,256]{1,0:T(8,128)S(1)}, s32[32,256]{1,0:T(8,128)}, u32[]{:S(2)}) copy-start(s32[32,256]{1,0:T(8,128)} %get-tuple-element.64) | copy-start | bytes 98308
  228.5 9.0 %copy-start.4 = (s32[256,4]{0,1:T(4,128)S(1)}, s32[256,4]{0,1:T(4,128)}, u32[]{:S(2)}) copy-start(s32[256,4]{0,1:T(4,128)} %param.13) | copy-start | bytes 12292
  260.2 24.9 %copy-start.6 = (f32[2,128]{1,0:T(2,128)}, f32[2,128]{1,0:T(2,128)S(1)}, u32[]{:S(2)}) copy-start(f32[2,128]{1,0:T(2,128)S(1)} %get-tuple-element.67) | copy-start | bytes 3076
  262.1 29.2 %all-to-all-start.2 = ((bf16[32,8,768]{2,1,0:T(8,128)(2,1)}), bf16[32,8,768]{2,1,0:T(8,128)(2,1)S(1)}, u32[]{:S(2)}, u32[]{:S(2)}) async-start(bf16[32,8,768]{2,1,0:T(8,128)(2,1)} %bitcast.14), calls=%async_computation.2 | async-start | bytes 786432 | tf_op jit(solution)/shard_map/all_to_all | solution.py:147
  291.3 14.8 %copy-start.5 = (bf16[256,768]{1,0:T(8,128)(2,1)S(1)}, bf16[256,768]{1,0:T(8,128)(2,1)}, u32[]{:S(2)}) copy-start(bf16[256,768]{1,0:T(8,128)(2,1)} %param.8) | copy-start | bytes 1179652
  291.3 14.8 %copy-start.7 = (f32[256,768]{1,0:T(8,128)S(1)}, f32[256,768]{1,0:T(8,128)}, u32[]{:S(2)}) copy-start(f32[256,768]{1,0:T(8,128)} %get-tuple-element.176) | copy-start | bytes 2359300
  291.3 286.4 %all-to-all-start.3 = ((bf16[32,1,128,768]{3,2,1,0:T(8,128)(2,1)}), bf16[32,1,128,768]{3,2,1,0:T(8,128)(2,1)}, u32[]{:S(2)}, u32[]{:S(2)}) async-start(bf16[32,1,128,768]{3,2,1,0:T(8,128)(2,1)} %copy.118), calls=%async_computation.3 | async-start | bytes 12582912 | tf_op jit(solution)/shard_map/all_to_all | solution.py:135
  301.4 79.2 %all-reduce.3.cloned.1.call-start = ((), (), s32[]{:S(2)}) async-start(), calls=%async_computation.4 | async-start | bytes 4718592 | tf_op jit(solution)/shard_map/psum | solution.py:16
  308.5 265.9 %all-reduce.5.cloned.1.call-start = ((), (), s32[]{:S(2)}) async-start(), calls=%async_computation.5 | async-start | bytes 4718592 | tf_op jit(solution)/shard_map/psum | solution.py:16
Sparse Core Ops, SparseCore 0:
  92.3 2.5 sort.72.cloned.1.call-done
  308.6 71.9 all-reduce.2
  384.2 190.1 all-reduce.4
  (1 shorter events, 0.0 us)
